TPU v7x, 512 devices: a whole 4x8x8 slice. The times are simulated.
512 devices in a mesh: member: 16 (over z, core), band: 32 (over y, x).
Axes of the slice: x: 4, y: 8, z: 8, core: 2. Of those that a mesh axis runs over, the one named last changes fastest.
Arguments:
- ensemble: bfloat16 [16, 2, 16, 128, 1440], P('member', None, None, 'band'), may hold values from -6 to 6
- member_weight: float32 [16], replicated, may hold values from 0.5 to 2
- member_of_slot: int32 [16], P('member'), may hold values from 0 to 15, each once
- halfwidth: int32 [16], replicated, may hold values from 1 to 4, as said below
- static_root: float32 [16, 16], replicated, may hold values from -1.5 to 1.5
- innovation: bfloat16 [2, 16, 128, 1440], P(None, None, 'band'), may hold values from -6 to 6
- precision: bfloat16 [16, 128, 1440], P(None, 'band'), may hold values from 0.1 to 3
Outputs:
- control_members: float32 [16, 16, 128, 1440], P('member', None, 'band')
- control_static: float32 [16, 128, 1440], P(None, 'band')
- increment: float32 [2, 16, 128, 1440], P(None, 'member', 'band')
Inputs may be any that keep to these rules, and one draw needn't show every extreme that they name: `member_of_slot`: each member appears in exactly one slot. `halfwidth`: some level has a half-width of exactly 4.
All inputs are finite; a program needn't handle non-finite values.
Results may differ from a plain program's by a relative error of at most 0.0062.
Values may be sent and summed in bfloat16 or wider, within the bound.
A program may use at most 64 MiB of HBM per device.

v0:
```python
import math
import jax
import jax.numpy as jnp
from jax import lax
from jax.sharding import PartitionSpec as P

ITERS = 2
HMAX = 4
LREACH = 18
ensemble_share = 0.8
static_share = 0.6
length_scale = 6.0


def with_halo(block, sides, width):
    for axis, dim in sides:
        count = lax.axis_size(axis)
        forward = [(i, i + 1) for i in range(count - 1)]
        backward = [(target, source) for source, target in forward]
        low = lax.ppermute(
            lax.slice_in_dim(block, block.shape[dim] - width, None, axis=dim), axis, forward
        )
        high = lax.ppermute(lax.slice_in_dim(block, 0, width, axis=dim), axis, backward)
        block = jnp.concatenate([low, block, high], axis=dim)
    return block


def lon_kernel(reach, width):
    rows_index = jnp.arange(width + 2 * reach, dtype=jnp.int32)[:, None]
    cols_index = jnp.arange(width, dtype=jnp.int32)[None, :]
    distance = jnp.abs(rows_index - reach - cols_index).astype(jnp.float32)
    values = jnp.exp(-0.5 * (distance / length_scale) ** 2) / (
        length_scale * math.sqrt(2.0 * math.pi)
    )
    return jnp.where(distance <= reach, values, jnp.zeros_like(values)).astype(jnp.bfloat16)


def smooth_longitude(field, reach, blocks):
    width = field.shape[-1] // blocks
    pieces = field.reshape(field.shape[:-1] + (blocks, width))
    before = jnp.roll(pieces, 1, axis=-2)[..., width - reach :]
    after = jnp.roll(pieces, -1, axis=-2)[..., :reach]
    window = jnp.concatenate([before, pieces, after], axis=-1)
    kernel = lon_kernel(reach, width)
    result = jnp.einsum("...bm,mo->...bo", window, kernel, preferred_element_type=jnp.float32)
    return result.reshape(field.shape).astype(jnp.bfloat16)


def taper_weights(halfwidth, reach):
    offsets = jnp.abs(jnp.arange(-reach, reach + 1, dtype=jnp.int32)).astype(jnp.float32)
    spans = halfwidth.astype(jnp.float32)[:, None] + 1.0
    return jnp.maximum(1.0 - offsets[None, :] / spans, 0.0) / spans


def localize(field, taper):
    smoothed = smooth_longitude(field.astype(jnp.bfloat16), LREACH, 3)
    padded = with_halo(smoothed, (("band", 2),), HMAX)
    row_count = field.shape[2]
    summed = jnp.zeros(field.shape, jnp.float32)
    for offset in range(2 * HMAX + 1):
        summed = summed + taper[:, offset][None, :, None, None] * padded[
            :, :, offset : offset + row_count, :
        ].astype(jnp.float32)
    return summed


def local_dot(first_members, second_members, first_static, second_static, groups):
    return jnp.sum(first_members * second_members) + jnp.sum(first_static * second_static) / groups


def shards(ensemble, member_weight, member_of_slot, halfwidth, static_root, innovation, precision):
    member_count = member_weight.shape[0]
    picker = (member_of_slot[:, None] == jnp.arange(member_count, dtype=jnp.int32)[None, :]).astype(
        jnp.float32
    )
    scaled = jnp.sum(picker * member_weight[None, :], axis=1)
    taper = taper_weights(halfwidth, HMAX)
    precise = precision.astype(jnp.float32)
    groups = lax.axis_size("member")
    level_share = precision.shape[0] // groups
    first_level = lax.axis_index("member") * level_share

    def adjoint(weighted):
        folded = scaled[:, None, None, None] * jnp.sum(
            ensemble.astype(jnp.float32) * weighted[None], axis=1
        )
        grad_members = ensemble_share * localize(folded, taper)
        grad_static = static_share * jnp.einsum(
            "ql,qyx->lyx", static_root, jnp.sum(weighted, axis=0), precision=lax.Precision.HIGHEST
        )
        return (grad_members, grad_static)

    res_members, res_static = adjoint(precise[None] * innovation.astype(jnp.float32))
    dir_members, dir_static = (res_members, res_static)
    sol_members = jnp.zeros_like(res_members)
    sol_static = jnp.zeros_like(res_static)
    increment = jnp.zeros((), jnp.float32)
    norm_now = lax.psum(
        local_dot(res_members, res_members, res_static, res_static, groups), ("member", "band")
    )
    for iteration in range(ITERS):
        localized = localize(dir_members, taper)
        partial_image = ensemble_share * jnp.sum(
            scaled[:, None, None, None, None] * ensemble.astype(jnp.float32) * localized[:, None],
            axis=0,
        )
        summed = lax.psum(partial_image, "member")
        static = jnp.einsum("lq,qyx->lyx", static_root, dir_static, precision=lax.Precision.HIGHEST)
        image = summed + static_share * static[None]
        hessian_weighted = precise[None] * image
        hessian_grad_members, hessian_grad_static = adjoint(hessian_weighted)
        hes_members, hes_static, image = (
            dir_members + hessian_grad_members,
            dir_static + hessian_grad_static,
            image,
        )
        curvature = lax.psum(
            local_dot(dir_members, hes_members, dir_static, hes_static, groups), ("member", "band")
        )
        alpha = norm_now / curvature
        sol_members = sol_members + alpha * dir_members
        sol_static = sol_static + alpha * dir_static
        increment = increment + alpha * image
        res_members = res_members - alpha * hes_members
        res_static = res_static - alpha * hes_static
        if iteration + 1 < ITERS:
            norm_next = lax.psum(
                local_dot(res_members, res_members, res_static, res_static, groups),
                ("member", "band"),
            )
            ratio = norm_next / norm_now
            dir_members = res_members + ratio * dir_members
            dir_static = res_static + ratio * dir_static
            norm_now = norm_next
    increment = lax.dynamic_slice_in_dim(increment, first_level, level_share, 1)
    return (sol_members, sol_static, increment)


def solution(mesh):
    return jax.shard_map(
        shards,
        mesh=mesh,
        in_specs=(
            P("member", None, None, "band", None),
            P(),
            P("member"),
            P(),
            P(),
            P(None, None, "band", None),
            P(None, "band", None),
        ),
        out_specs=(
            P("member", None, "band", None),
            P(None, "band", None),
            P(None, "member", "band", None),
        ),
        check_vma=False,
    )
```

profile of v0, /device:TPU:1, one launch (start us, length us, event | category | flops | bytes accessed | tf_op | source)
XLA Modules:
  0.0 658.5 jit_solution(16516160532751708579)
XLA Ops:
  10.1 1.6 fusion.13
  14.2 4.0 collective-permute-start
  20.8 3.8 collective-permute-done.1
  26.7 4.0 collective-permute-start.2
  33.3 4.1 collective-permute-done.3
  38.1 1.8 fusion.10
  41.3 126.7 %all-reduce.4.cloned.1.call-done = f32[2,16,4,1440]{3,2,1,0:T(4,128)} async-done(((f32[2,16,4,1440]{3,2,1,0:T(4,128)}), f32[2,16,4,1440]{3,2,1,0:T(4,128)}) %all-reduce.4.cloned.1.call-update) | async-done | bytes 737296 | tf_op jit(solution)/shard_map/psum | solution.py:107
  168.0 1.7 multiply_reduce_fusion.1
  172.6 3.1 collective-permute-start.4
  179.7 3.3 collective-permute-done.5
  184.0 2.1 multiply_reduce_fusion.4
  187.4 101.5 %all-reduce = (f32[]{:T(128)}, f32[]{:T(128)}) all-reduce(f32[]{:T(128)S(6)} %add.217, f32[]{:T(128)S(6)} %add.238), channel_id=1, replica_groups=mesh['member'=16,'band'=32] {'member','band'}, use_global_device_ids=true, to_apply=%region_5.6 | all-reduce | flops 2 | bytes 16 | tf_op jit(solution)/shard_map/psum | solution.py:98
  292.7 94.9 %psum.45 = f32[]{:T(128)} all-reduce(f32[]{:T(128)S(6)} %add.239), channel_id=1, replica_groups=mesh['member'=16,'band'=32] {'member','band'}, use_global_device_ids=true, to_apply=%region_14.15 | all-reduce | flops 1 | bytes 8 | tf_op jit(solution)/shard_map/psum | solution.py:127
  394.0 3.7 collective-permute-start.6
  399.0 2.2 collective-permute-done.6
  401.3 3.8 collective-permute-done.7
  405.8 1.8 fusion.12
  409.1 116.4 %all-reduce.6.cloned.1.call-done = f32[2,16,4,1440]{3,2,1,0:T(4,128)} async-done(((f32[2,16,4,1440]{3,2,1,0:T(4,128)}), f32[2,16,4,1440]{3,2,1,0:T(4,128)}) %all-reduce.6.cloned.1.call-update) | async-done | bytes 737296 | tf_op jit(solution)/shard_map/psum | solution.py:107
  525.5 1.8 multiply_reduce_fusion
  531.2 3.1 collective-permute-start.8
  537.8 3.9 collective-permute-done.9
  542.7 2.0 fusion.39
  545.3 101.3 %psum.47 = f32[]{:T(128)} all-reduce(f32[]{:T(128)S(6)} %add.262), channel_id=1, replica_groups=mesh['member'=16,'band'=32] {'member','band'}, use_global_device_ids=true, to_apply=%region_20.21 | all-reduce | flops 1 | bytes 8 | tf_op jit(solution)/shard_map/psum | solution.py:117
  647.9 1.4 fusion.92
  (153 shorter events, 40.0 us)
Async XLA Ops:
  7.2 32.8 %copy-start = (f32[16,16]{1,0:T(8,128)S(1)}, f32[16,16]{1,0:T(8,128)}, u32[]{:S(2)}) copy-start(f32[16,16]{1,0:T(8,128)} %param.11) | copy-start | bytes 3076
  7.2 160.8 %all-reduce.4.cloned.1.call-start = ((), (), s32[]{:S(2)}) async-start(), calls=%async_computation | async-start | bytes 1572864 | tf_op jit(solution)/shard_map/psum | solution.py:107
  12.9 158.4 %copy-start.25 = (s32[516]{0:T(1024)}, s32[516]{0:T(1024)S(1)}, u32[]{:S(2)}) copy-start(s32[516]{0:T(1024)S(1)} %iota_add_fusion) | copy-start | bytes 6196
  14.2 6.6 collective-permute-start
  18.2 6.4 collective-permute-start.1
  19.6 17.9 %copy-start.4 = (f32[16]{0:T(128)}, f32[16]{0:T(128)S(1)}, u32[]{:S(2)}) copy-start(f32[16]{0:T(128)S(1)} %get-tuple-element.60) | copy-start | bytes 196
  19.6 17.9 %copy-start.7 = (f32[16]{0:T(128)}, f32[16]{0:T(128)S(1)}, u32[]{:S(2)}) copy-start(f32[16]{0:T(128)S(1)} %get-tuple-element.61) | copy-start | bytes 196
  19.6 17.9 %copy-start.10 = (f32[16]{0:T(128)}, f32[16]{0:T(128)S(1)}, u32[]{:S(2)}) copy-start(f32[16]{0:T(128)S(1)} %get-tuple-element.62) | copy-start | bytes 196
  19.6 17.9 %copy-start.13 = (f32[16]{0:T(128)}, f32[16]{0:T(128)S(1)}, u32[]{:S(2)}) copy-start(f32[16]{0:T(128)S(1)} %get-tuple-element.63) | copy-start | bytes 196
  19.6 17.9 %copy-start.16 = (f32[16]{0:T(128)}, f32[16]{0:T(128)S(1)}, u32[]{:S(2)}) copy-start(f32[16]{0:T(128)S(1)} %get-tuple-element.64) | copy-start | bytes 196
  19.6 17.9 %copy-start.19 = (f32[16]{0:T(128)}, f32[16]{0:T(128)S(1)}, u32[]{:S(2)}) copy-start(f32[16]{0:T(128)S(1)} %get-tuple-element.65) | copy-start | bytes 196
  19.6 17.9 %copy-start.22 = (f32[16]{0:T(128)}, f32[16]{0:T(128)S(1)}, u32[]{:S(2)}) copy-start(f32[16]{0:T(128)S(1)} %get-tuple-element.66) | copy-start | bytes 196
  26.7 6.6 %collective-permute-start.2 = (bf16[1,16,4,1440]{3,1,2,0:T(8,128)(2,1)S(1)}, bf16[1,16,4,1440]{3,1,2,0:T(8,128)(2,1)S(1)}, u32[]{:S(2)}, u32[]{:S(2)}) collective-permute-start(bf16[1,16,4,1440]{3,1,2,0:T(8,128)(2,1)S(1)} %convert_element_type.392), channel_id=1, source_target_pairs={{0,1},{1,2},{2,3},{3,4},{4,5},{5,6},{6,7},{7,8},{8,9},{9,10},{10,1... | collective-permute-start | bytes 552968 | tf_op jit(solution)/shard_map/ppermute | solution.py:20
  31.0 6.4 collective-permute-start.3
  39.9 485.6 %all-reduce.6.cloned.1.call-start = ((), (), s32[]{:S(2)}) async-start(), calls=%async_computation.1 | async-start | bytes 1572864 | tf_op jit(solution)/shard_map/psum | solution.py:107
  172.6 7.1 %collective-permute-start.4 = (bf16[1,16,4,1440]{3,1,2,0:T(8,128)(2,1)S(1)}, bf16[1,16,4,1440]{3,1,2,0:T(8,128)(2,1)S(1)}, u32[]{:S(2)}, u32[]{:S(2)}) collective-permute-start(bf16[1,16,4,1440]{3,1,2,0:T(8,128)(2,1)S(1)} %convert_element_type.405), channel_id=1, source_target_pairs={{0,1},{1,2},{2,3},{3,4},{4,5},{5,6},{6,7},{7,8},{8,9},{9,10},{10,1... | collective-permute-start | bytes 552968 | tf_op jit(solution)/shard_map/ppermute | solution.py:20
  175.7 7.3 %collective-permute-start.5 = (bf16[1,16,4,1440]{3,1,2,0:T(8,128)(2,1)S(1)}, bf16[1,16,4,1440]{3,1,2,0:T(8,128)(2,1)}, u32[]{:S(2)}, u32[]{:S(2)}) collective-permute-start(bf16[1,16,4,1440]{3,1,2,0:T(8,128)(2,1)S(1)} %convert_element_type.405), channel_id=1, source_target_pairs={{1,0},{2,1},{3,2},{4,3},{5,4},{6,5},{7,6},{8,7},{9,8},{10,9},{11,1... | collective-permute-start | bytes 552968 | tf_op jit(solution)/shard_map/ppermute | solution.py:23
  394.0 11.1 %copy-start.5 = (f32[16]{0:T(128)S(1)}, f32[16]{0:T(128)}, u32[]{:S(2)}) copy-start(f32[16]{0:T(128)} %copy-done.4) | copy-start | bytes 196
  394.0 11.1 %copy-start.8 = (f32[16]{0:T(128)S(1)}, f32[16]{0:T(128)}, u32[]{:S(2)}) copy-start(f32[16]{0:T(128)} %copy-done.7) | copy-start | bytes 196
  394.0 11.1 %copy-start.11 = (f32[16]{0:T(128)S(1)}, f32[16]{0:T(128)}, u32[]{:S(2)}) copy-start(f32[16]{0:T(128)} %copy-done.10) | copy-start | bytes 196
  394.0 7.2 %collective-permute-start.6 = (bf16[1,16,4,1440]{3,1,2,0:T(8,128)(2,1)S(1)}, bf16[1,16,4,1440]{3,1,2,0:T(8,128)(2,1)S(1)}, u32[]{:S(2)}, u32[]{:S(2)}) collective-permute-start(bf16[1,16,4,1440]{3,1,2,0:T(8,128)(2,1)S(1)} %convert_element_type.417), channel_id=1, source_target_pairs={{0,1},{1,2},{2,3},{3,4},{4,5},{5,6},{6,7},{7,8},{8,9},{9,10},{10,1... | collective-permute-start | bytes 552968 | tf_op jit(solution)/shard_map/ppermute | solution.py:20
  397.7 7.4 %collective-permute-start.7 = (bf16[1,16,4,1440]{3,1,2,0:T(8,128)(2,1)S(1)}, bf16[1,16,4,1440]{3,1,2,0:T(8,128)(2,1)S(1)}, u32[]{:S(2)}, u32[]{:S(2)}) collective-permute-start(bf16[1,16,4,1440]{3,1,2,0:T(8,128)(2,1)S(1)} %convert_element_type.417), channel_id=1, source_target_pairs={{1,0},{2,1},{3,2},{4,3},{5,4},{6,5},{7,6},{8,7},{9,8},{10,9},{11,1... | collective-permute-start | bytes 552968 | tf_op jit(solution)/shard_map/ppermute | solution.py:23
  531.2 6.5 collective-permute-start.8
  534.3 7.3 %collective-permute-start.9 = (bf16[1,16,4,1440]{3,1,2,0:T(8,128)(2,1)S(1)}, bf16[1,16,4,1440]{3,1,2,0:T(8,128)(2,1)}, u32[]{:S(2)}, u32[]{:S(2)}) collective-permute-start(bf16[1,16,4,1440]{3,1,2,0:T(8,128)(2,1)S(1)} %convert_element_type.430), channel_id=1, source_target_pairs={{1,0},{2,1},{3,2},{4,3},{5,4},{6,5},{7,6},{8,7},{9,8},{10,9},{11,1... | collective-permute-start | bytes 552968 | tf_op jit(solution)/shard_map/ppermute | solution.py:23
  (17 other events, 101.0 us)
Sparse Core Ops, SparseCore 0:
  40.1 127.9 all-reduce.3
  407.7 117.7 all-reduce.5
where the time goes:
time: 659 us; the launch traced here: 658 us
  blocking collectives  298 us (45%)
  waiting for transfers between devices  266 us (40%)
  between operations  24.5 us (4%)
  starting transfers between devices  24.4 us (4%)
  other arithmetic  23.4 us (4%)
  local copies, waits for them, and re-layouts  13.4 us (2%)
  matrix products  8.49 us (1%)
    psum x2, waiting for transfers between devices, shards(): summed = lax.psum(partial_image, 'member')  243 us
    psum x2, blocking collectives, shards(): lax.psum(local_dot(res_members, res_members, res_static, res_static, grou...  196 us
    psum x1, blocking collectives, shards(): lax.psum(local_dot(dir_members, hes_members, dir_static, hes_static, grou...  101 us
    ppermute x5, waiting for transfers between devices, with_halo(): lax.ppermute(lax.slice_in_dim(block, 0, width, axis=dim), axis, backward)  18.7 us
    ppermute x5, starting transfers between devices, with_halo(): lax.ppermute(lax.slice_in_dim(block, block.shape[dim] - width, None, axis...  17.9 us
  transfers between devices with their start and end apart: 12, of which 11 were waited for; matrix products, arithmetic and copies ran while one was open for 1% of the time, Pallas kernels for 0%

commit v1 on v0

--- a/solution.py
+++ b/solution.py
@@ -96,7 +96,8 @@
     sol_static = jnp.zeros_like(res_static)
     increment = jnp.zeros((), jnp.float32)
     norm_now = lax.psum(
-        local_dot(res_members, res_members, res_static, res_static, groups), ("member", "band")
+        lax.psum(local_dot(res_members, res_members, res_static, res_static, groups), "member"),
+        "band",
     )
     for iteration in range(ITERS):
         localized = localize(dir_members, taper)

time: 659 us -> 754 us (1.14)
  blocking collectives: 298 us -> 392 us
    psum x1 -> x2, blocking collectives: 101 us -> 202 us  [shards(): lax.psum(local_dot(dir_members, hes_members, dir_static, hes_static, grou...]
    psum x2, blocking collectives: 196 us -> 134 us  [shards(): lax.psum(local_dot(res_members, res_members, res_static, res_static, grou...]
    psum x0 -> x1, blocking collectives: none -> 56.9 us  [shards(): lax.psum(lax.psum(local_dot(res_members, res_members, res_static, res_sta...]
where the time goes in v1:
time: 754 us; the launch traced here: 753 us
  blocking collectives  392 us (52%)
  waiting for transfers between devices  267 us (35%)
  between operations  24.5 us (3%)
  starting transfers between devices  24.4 us (3%)
  other arithmetic  23.3 us (3%)
  local copies, waits for them, and re-layouts  13.4 us (2%)
  matrix products  8.45 us (1%)
    psum x2, waiting for transfers between devices, shards(): summed = lax.psum(partial_image, 'member')  243 us
    psum x2, blocking collectives, shards(): lax.psum(local_dot(dir_members, hes_members, dir_static, hes_static, grou...  202 us
    psum x2, blocking collectives, shards(): lax.psum(local_dot(res_members, res_members, res_static, res_static, grou...  134 us
    psum x1, blocking collectives, shards(): lax.psum(lax.psum(local_dot(res_members, res_members, res_static, res_sta...  56.9 us
    ppermute x5, waiting for transfers between devices, with_halo(): lax.ppermute(lax.slice_in_dim(block, 0, width, axis=dim), axis, backward)  18.8 us
    ppermute x5, starting transfers between devices, with_halo(): lax.ppermute(lax.slice_in_dim(block, block.shape[dim] - width, None, axis...  17.9 us
  transfers between devices with their start and end apart: 12, of which 11 were waited for; matrix products, arithmetic and copies ran while one was open for 1% of the time, Pallas kernels for 0%

profile of v1, /device:TPU:1, one launch (start us, length us, event | category | flops | bytes accessed | tf_op | source)
XLA Modules:
  0.0 753.2 jit_solution(16499442976550567291)
XLA Ops:
  14.2 4.0 collective-permute-start
  20.8 3.8 collective-permute-done.1
  26.7 4.0 collective-permute-start.2
  33.3 4.1 collective-permute-done.3
  38.1 1.8 fusion.10
  41.3 126.7 %all-reduce.3.cloned.1.call-done = f32[2,16,4,1440]{3,2,1,0:T(4,128)} async-done(((f32[2,16,4,1440]{3,2,1,0:T(4,128)}), f32[2,16,4,1440]{3,2,1,0:T(4,128)}) %all-reduce.3.cloned.1.call-update) | async-done | bytes 737296 | tf_op jit(solution)/shard_map/psum | solution.py:108
  168.0 1.7 multiply_reduce_fusion.1
  172.6 3.1 collective-permute-start.4
  179.6 3.4 collective-permute-done.5
  184.0 2.0 multiply_reduce_fusion.4
  187.3 25.4 %psum.49 = f32[]{:T(128)} all-reduce(f32[]{:T(128)S(6)} %add.219), channel_id=1, replica_groups=mesh['member'=16,'band'=32] {'member'}, use_global_device_ids=true, to_apply=%region_5.6 | all-reduce | flops 1 | bytes 8 | tf_op jit(solution)/shard_map/psum | solution.py:99
  212.7 100.4 %psum.52 = f32[]{:T(128)} all-reduce(f32[]{:T(128)S(6)} %add.240), channel_id=1, replica_groups=mesh['member'=16,'band'=32] {'member','band'}, use_global_device_ids=true, to_apply=%region_12.13 | all-reduce | flops 1 | bytes 8 | tf_op jit(solution)/shard_map/psum | solution.py:118
  313.1 56.9 %psum.50 = f32[]{:T(128)} all-reduce(f32[]{:T(128)} %psum.49), channel_id=1, replica_groups=mesh['member'=16,'band'=32] {'band'}, use_global_device_ids=true, to_apply=%region_6.7 | all-reduce | flops 1 | bytes 8 | tf_op jit(solution)/shard_map/psum | solution.py:98
  373.8 108.2 %psum.53 = f32[]{:T(128)} all-reduce(f32[]{:T(128)S(6)} %add.241), channel_id=1, replica_groups=mesh['member'=16,'band'=32] {'member','band'}, use_global_device_ids=true, to_apply=%region_15.16 | all-reduce | flops 1 | bytes 8 | tf_op jit(solution)/shard_map/psum | solution.py:128
  488.4 3.7 collective-permute-start.6
  493.4 2.3 collective-permute-done.6
  495.7 3.8 collective-permute-done.7
  500.2 1.8 fusion.12
  503.5 116.7 %all-reduce.5.cloned.1.call-done = f32[2,16,4,1440]{3,2,1,0:T(4,128)} async-done(((f32[2,16,4,1440]{3,2,1,0:T(4,128)}), f32[2,16,4,1440]{3,2,1,0:T(4,128)}) %all-reduce.5.cloned.1.call-update) | async-done | bytes 737296 | tf_op jit(solution)/shard_map/psum | solution.py:108
  620.2 1.8 multiply_reduce_fusion
  625.9 3.1 collective-permute-start.8
  632.5 3.9 collective-permute-done.9
  637.4 2.0 fusion.39
  640.0 101.3 %psum.55 = f32[]{:T(128)} all-reduce(f32[]{:T(128)S(6)} %add.264), channel_id=1, replica_groups=mesh['member'=16,'band'=32] {'member','band'}, use_global_device_ids=true, to_apply=%region_21.22 | all-reduce | flops 1 | bytes 8 | tf_op jit(solution)/shard_map/psum | solution.py:118
  (155 shorter events, 43.0 us)
Async XLA Ops:
  7.2 32.8 %copy-start = (f32[16,16]{1,0:T(8,128)S(1)}, f32[16,16]{1,0:T(8,128)}, u32[]{:S(2)}) copy-start(f32[16,16]{1,0:T(8,128)} %param.11) | copy-start | bytes 3076
  7.2 160.8 %all-reduce.3.cloned.1.call-start = ((), (), s32[]{:S(2)}) async-start(), calls=%async_computation | async-start | bytes 1572864 | tf_op jit(solution)/shard_map/psum | solution.py:108
  12.9 158.4 %copy-start.25 = (s32[516]{0:T(1024)}, s32[516]{0:T(1024)S(1)}, u32[]{:S(2)}) copy-start(s32[516]{0:T(1024)S(1)} %iota_add_fusion) | copy-start | bytes 6196
  14.2 6.6 collective-permute-start
  18.2 6.4 collective-permute-start.1
  19.6 17.9 %copy-start.4 = (f32[16]{0:T(128)}, f32[16]{0:T(128)S(1)}, u32[]{:S(2)}) copy-start(f32[16]{0:T(128)S(1)} %get-tuple-element.58) | copy-start | bytes 196
  19.6 17.9 %copy-start.7 = (f32[16]{0:T(128)}, f32[16]{0:T(128)S(1)}, u32[]{:S(2)}) copy-start(f32[16]{0:T(128)S(1)} %get-tuple-element.59) | copy-start | bytes 196
  19.6 17.9 %copy-start.10 = (f32[16]{0:T(128)}, f32[16]{0:T(128)S(1)}, u32[]{:S(2)}) copy-start(f32[16]{0:T(128)S(1)} %get-tuple-element.60) | copy-start | bytes 196
  19.6 17.9 %copy-start.13 = (f32[16]{0:T(128)}, f32[16]{0:T(128)S(1)}, u32[]{:S(2)}) copy-start(f32[16]{0:T(128)S(1)} %get-tuple-element.61) | copy-start | bytes 196
  19.6 17.9 %copy-start.16 = (f32[16]{0:T(128)}, f32[16]{0:T(128)S(1)}, u32[]{:S(2)}) copy-start(f32[16]{0:T(128)S(1)} %get-tuple-element.62) | copy-start | bytes 196
  19.6 17.9 %copy-start.19 = (f32[16]{0:T(128)}, f32[16]{0:T(128)S(1)}, u32[]{:S(2)}) copy-start(f32[16]{0:T(128)S(1)} %get-tuple-element.63) | copy-start | bytes 196
  19.6 17.9 %copy-start.22 = (f32[16]{0:T(128)}, f32[16]{0:T(128)S(1)}, u32[]{:S(2)}) copy-start(f32[16]{0:T(128)S(1)} %get-tuple-element.64) | copy-start | bytes 196
  26.7 6.6 collective-permute-start.2
  31.0 6.4 collective-permute-start.3
  39.9 580.3 %all-reduce.5.cloned.1.call-start = ((), (), s32[]{:S(2)}) async-start(), calls=%async_computation.1 | async-start | bytes 1572864 | tf_op jit(solution)/shard_map/psum | solution.py:108
  172.6 7.0 collective-permute-start.4
  175.7 7.3 collective-permute-start.5
  488.3 11.1 %copy-start.5 = (f32[16]{0:T(128)S(1)}, f32[16]{0:T(128)}, u32[]{:S(2)}) copy-start(f32[16]{0:T(128)} %copy-done.4) | copy-start | bytes 196
  488.3 11.1 %copy-start.8 = (f32[16]{0:T(128)S(1)}, f32[16]{0:T(128)}, u32[]{:S(2)}) copy-start(f32[16]{0:T(128)} %copy-done.7) | copy-start | bytes 196
  488.3 11.1 %copy-start.11 = (f32[16]{0:T(128)S(1)}, f32[16]{0:T(128)}, u32[]{:S(2)}) copy-start(f32[16]{0:T(128)} %copy-done.10) | copy-start | bytes 196
  488.4 7.3 collective-permute-start.6
  492.1 7.4 collective-permute-start.7
  625.9 6.5 collective-permute-start.8
  629.0 7.3 collective-permute-start.9
  (17 other events, 100.9 us)
Sparse Core Ops, SparseCore 0:
  40.1 127.9 all-reduce.2
  502.1 118.0 all-reduce.4
